TPU v7x, 32 devices: a whole 2x2x4 slice. The times are simulated.
32 devices in a mesh: row: 4 (over y, x), col: 4 (over z), depth: 2 (over core).
Axes of the slice: x: 2, y: 2, z: 4, core: 2. Of those that a mesh axis runs over, the one named last changes fastest.
Arguments:
- features: bfloat16 [4096, 768], P(('row', 'col', 'depth')), may hold values from -6 to 6
- w_value: bfloat16 [768, 3072], replicated, may hold values from -0.21875 to 0.21875
- att_src: bfloat16 [4, 768], replicated, may hold values from -12 to 12
- att_dst: bfloat16 [4, 768], replicated, may hold values from -0.3984375 to 0.3984375
- tile_cols: int32 [32, 8], P('row'), may hold values from 0 to 31, as said below
- tile_count: int32 [32], P('row'), may hold values from 2 to 8, as said below
- neighbours: int32 [4096, 16], P('row'), may hold values from 0 to 4095, as said below
Outputs:
- mixed: bfloat16 [4096, 768], P(('row', 'col', 'depth'))
Inputs may be any that keep to these rules, and one draw needn't show every extreme that they name: tile_cols[t, 0] is t itself and the 8 tiles of a row tile are distinct. Tile c lies in run c // 2 and in column group (c // 2) % 4. Of the 8 tiles of one row tile at most 2 lie in one column group, and some row tile lists 2 of one group among its first tile_count tiles. Every tile of row tile t lies in t's run or in one of the 7 runs that follow it, cyclically over 16 runs, and some listed tile lies in the last of these. `tile_count`: some row tile lists all 8. The 16 neighbours of node i are distinct, differ from i, and lie in tiles tile_cols[i // 128, s] with s < tile_count[i // 128].
All inputs are finite; a program needn't handle non-finite values.
Results may differ from a plain program's by a relative error of at most 0.0059.
Values may be sent and summed in bfloat16 or wider, within the bound.
No kernel may reach another device: no remote copies, remote signals or barrier semaphores. Data moves between devices by JAX's collectives and lax.ppermute only.
A program may use at most 64 MiB of HBM per device.

v0:
```python
import functools

import jax
import jax.numpy as jnp
from jax import lax
from jax.experimental import pallas as pl
from jax.experimental.pallas import tpu as pltpu
from jax.sharding import PartitionSpec as P


AXES = ("row", "col", "depth")
LEAK_SLOPE = 0.2
NEG_BIG = -1e30
VM = pl.BlockSpec(memory_space=pltpu.VMEM)
SM = pl.BlockSpec(memory_space=pltpu.SMEM)
HBM = pl.BlockSpec(memory_space=pltpu.HBM)
ANY = pl.BlockSpec(memory_space=pl.ANY)
F32 = jnp.float32
BF16 = jnp.bfloat16


def ahead(array, axis, by):
    length = lax.axis_size(axis)
    return lax.ppermute(array, axis, [((i + by) % length, i) for i in range(length)])


def place_of_device():
    depths = lax.axis_size("depth")
    chip = lax.axis_index("row") * lax.axis_size("col") + lax.axis_index("col")
    depth = lax.axis_index("depth")
    return chip, depth, lax.axis_index("col") * depths + depth


def window_tile(tile, chip, depth, chips, depths):
    step = tile // depths - chip
    step = jnp.where(step < 0, step + chips, step)
    side = tile % depths - depth
    side = jnp.where(side < 0, side + depths, side)
    return step * depths + side


def slot_tiles(cols_ref, count_ref, chips, depths):
    chip, depth, own = place_of_device()
    count = count_ref[own]
    return [
        jnp.where(s < count, window_tile(cols_ref[own, s], chip, depth, chips, depths), 0)
        for s in range(cols_ref.shape[1])
    ], count


def score_kernel(features_ref, w_ref, src_ref, dst_ref, source_ref, target_ref):
    heads, width = src_ref.shape
    contract_last = (((1,), (1,)), ((), ()))
    for h in range(heads):
        value = jnp.dot(
            features_ref[...],
            w_ref[:, h * width : (h + 1) * width],
            preferred_element_type=F32,
        ).astype(BF16)
        source = lax.dot_general(value, src_ref[...], contract_last, preferred_element_type=F32)
        target = lax.dot_general(dst_ref[...], value, contract_last, preferred_element_type=F32)
        source_ref[:, h : h + 1] = source[:, h : h + 1]
        target_ref[h : h + 1, :] = target[h : h + 1, :]


def link_kernel(cols_ref, count_ref, near_ref, link_ref, near_scratch, sem):
    tile, near_count = near_scratch.shape
    _, _, own = place_of_device()
    copy = pltpu.make_async_copy(near_ref.at[pl.ds(own * tile, tile)], near_scratch, sem)
    copy.start()
    copy.wait()
    near = near_scratch[...]
    near_tile = near // tile
    bit = jnp.zeros(near.shape, jnp.int32)
    for s in range(cols_ref.shape[1]):
        listed = jnp.where(s < count_ref[own], cols_ref[own, s], -1)
        bit = jnp.where(near_tile == listed, 1 << s, bit)
    spot = near % tile
    lane = lax.broadcasted_iota(jnp.int32, (tile, tile), 1)
    row = lax.broadcasted_iota(jnp.int32, (tile, tile), 0)
    link = jnp.where(lane == row, 1, 0)
    for k in range(near_count):
        link = link | jnp.where(spot[:, k : k + 1] == lane, bit[:, k : k + 1], 0)
    link_ref[...] = link


def coef_kernel(chips, depths, cols_ref, count_ref, source_ref, link_ref, *refs):
    target_refs, (coef_ref, all_targets, targets) = refs[:-3], refs[-3:]
    steps, heads, tile = target_refs[0].shape
    for i, ref in enumerate(target_refs):
        part, side = i // depths, i % depths
        for k in range(steps):
            all_targets[(part * steps + k) * depths + side] = ref[k]
    places, _ = slot_tiles(cols_ref, count_ref, chips, depths)
    slots = len(places)
    for s in range(slots):
        targets[:, s * tile : (s + 1) * tile] = all_targets[places[s]]
    rows = source_ref.shape[0]
    block = 16

    def step(b, carry):
        at = pl.ds(pl.multiple_of(b * block, block), block)
        link = link_ref[at, :]
        linked = jnp.concatenate([link & (1 << s) for s in range(slots)], axis=1) != 0
        for h in range(heads):
            logits = source_ref[at, h : h + 1] + targets[h : h + 1, :]
            logits = jnp.where(linked, jnp.maximum(logits, LEAK_SLOPE * logits), NEG_BIG)
            peak = jnp.max(logits, axis=1, keepdims=True)
            weights = jnp.exp(logits - peak)
            total = jnp.sum(weights, axis=1, keepdims=True)
            out = pl.ds(pl.multiple_of(h * rows + b * block, block), block)
            coef_ref[out, :] = (weights * (1.0 / total)).astype(BF16)
        return carry

    lax.fori_loop(0, rows // block, step, 0)


def early_kernel(chips, depths, late, cols_ref, count_ref, coef_ref, *refs):
    feature_refs, (out_ref, picked, sems) = refs[:-3], refs[-3:]
    tile = feature_refs[0].shape[0]
    tiles = len(feature_refs) + late
    places, _ = slot_tiles(cols_ref, count_ref, chips, depths)
    for s, place in enumerate(places):
        at = picked.at[pl.ds(s * tile, tile)]

        @pl.when(place >= tiles - late)
        def _(at=at):
            at[...] = jnp.zeros(at.shape, at.dtype)

        for w, ref in enumerate(feature_refs):

            @pl.when(place == w)
            def _(ref=ref, at=at, s=s):
                pltpu.make_async_copy(ref, at, sems.at[s]).start()

    for s, place in enumerate(places):

        @pl.when(place < tiles - late)
        def _(s=s):
            at = picked.at[pl.ds(s * tile, tile)]
            pltpu.make_async_copy(feature_refs[0], at, sems.at[s]).wait()

    out_ref[...] = jnp.dot(coef_ref[...], picked[...], preferred_element_type=F32)


def late_kernel(chips, depths, cols_ref, count_ref, gathered_ref, coef_ref, w_ref, *refs):
    feature_refs, (out_ref, total_ref) = refs[:-2], refs[-2:]
    tile, width = feature_refs[0].shape
    rows = out_ref.shape[0]
    heads = coef_ref.shape[0] // rows
    tiles = 2 * lax.axis_size("col") * depths
    places, _ = slot_tiles(cols_ref, count_ref, chips, depths)
    total_ref[...] = gathered_ref[...]
    for s, place in enumerate(places):
        for w, ref in enumerate(feature_refs):

            @pl.when(place == tiles - len(feature_refs) + w)
            def _(ref=ref, s=s):
                total_ref[...] += jnp.dot(
                    coef_ref[:, s * tile : (s + 1) * tile], ref[...], preferred_element_type=F32
                )

    total = None
    for h in range(heads):
        part = jnp.dot(
            total_ref[h * rows : (h + 1) * rows].astype(BF16),
            w_ref[:, h * width : (h + 1) * width],
            preferred_element_type=F32,
        )
        total = part if total is None else total + part
    mixed = total * (1.0 / heads)
    out_ref[...] = jnp.where(mixed > 0, mixed, jnp.exp(mixed) - 1.0).astype(out_ref.dtype)


def scores_of(features, w_value, att_src, att_dst):
    rows, heads = features.shape[0], att_src.shape[0]
    return pl.pallas_call(
        score_kernel,
        out_shape=(
            jax.ShapeDtypeStruct((rows, heads), F32),
            jax.ShapeDtypeStruct((heads, rows), F32),
        ),
        in_specs=[VM] * 4,
        out_specs=(VM, VM),
        cost_estimate=pl.CostEstimate(
            flops=2 * rows * w_value.size, bytes_accessed=2 * w_value.size, transcendentals=0
        ),
        compiler_params=pltpu.CompilerParams(vmem_limit_bytes=16 << 20),
        name="scores",
    )(features, w_value, att_src, att_dst)


def links_of(tile_cols, tile_count, neighbours, tile):
    return pl.pallas_call(
        link_kernel,
        out_shape=jax.ShapeDtypeStruct((tile, tile), jnp.int32),
        in_specs=[SM, SM, HBM],
        out_specs=VM,
        scratch_shapes=[
            pltpu.VMEM((tile, neighbours.shape[1]), jnp.int32),
            pltpu.SemaphoreType.DMA,
        ],
        cost_estimate=pl.CostEstimate(
            flops=8 * tile * tile * neighbours.shape[1],
            bytes_accessed=4 * tile * tile,
            transcendentals=0,
        ),
        compiler_params=pltpu.CompilerParams(vmem_limit_bytes=4 << 20),
        name="links",
    )(tile_cols, tile_count, neighbours)


def coefs_of(chips, depths, tile_cols, tile_count, source, link, *targets):
    rows, heads = source.shape
    slots = tile_cols.shape[1]
    tile = link.shape[1]
    tiles = len(targets) * targets[0].shape[0]
    return pl.pallas_call(
        functools.partial(coef_kernel, chips, depths),
        out_shape=jax.ShapeDtypeStruct((heads * rows, slots * tile), BF16),
        in_specs=[SM, SM] + [VM] * (2 + len(targets)),
        out_specs=VM,
        scratch_shapes=[pltpu.VMEM((tiles, heads, tile), F32), pltpu.VMEM((heads, slots * tile), F32)],
        cost_estimate=pl.CostEstimate(
            flops=8 * heads * rows * slots * tile,
            bytes_accessed=4 * heads * rows * slots * tile,
            transcendentals=heads * rows * slots * tile,
        ),
        compiler_params=pltpu.CompilerParams(vmem_limit_bytes=8 << 20),
        name="coef",
    )(tile_cols, tile_count, source, link, *targets)


def early_of(chips, depths, late, tile_cols, tile_count, coef, *window):
    tile, width = window[0].shape
    slots = tile_cols.shape[1]
    return pl.pallas_call(
        functools.partial(early_kernel, chips, depths, late),
        out_shape=jax.ShapeDtypeStruct((coef.shape[0], width), F32),
        in_specs=[SM, SM, VM] + [ANY] * len(window),
        out_specs=VM,
        scratch_shapes=[pltpu.VMEM((slots * tile, width), BF16), pltpu.SemaphoreType.DMA((slots,))],
        cost_estimate=pl.CostEstimate(
            flops=2 * coef.size * width, bytes_accessed=6 * coef.size, transcendentals=0
        ),
        compiler_params=pltpu.CompilerParams(vmem_limit_bytes=12 << 20),
        name="early",
    )(tile_cols, tile_count, coef, *window)


def late_of(chips, depths, tile_cols, tile_count, gathered, coef, w_value, *window):
    tile, width = window[0].shape
    return pl.pallas_call(
        functools.partial(late_kernel, chips, depths),
        out_shape=jax.ShapeDtypeStruct((tile, width), BF16),
        in_specs=[SM, SM] + [VM] * (3 + len(window)),
        out_specs=VM,
        scratch_shapes=[pltpu.VMEM(gathered.shape, F32)],
        cost_estimate=pl.CostEstimate(
            flops=2 * tile * w_value.size, bytes_accessed=4 * gathered.size, transcendentals=tile * width
        ),
        compiler_params=pltpu.CompilerParams(vmem_limit_bytes=16 << 20),
        name="late",
    )(tile_cols, tile_count, gathered, coef, w_value, *window)


def on_device(features, w_value, att_src, att_dst, tile_cols, tile_count, neighbours):
    tile = features.shape[0]
    cols = lax.axis_size("col")
    depths = lax.axis_size("depth")
    chips = lax.axis_size("row") * cols
    cores = range(1, depths)

    near = [features] + [ahead(features, AXES, k * depths) for k in range(1, cols)]
    far = [ahead(x, "row", 1) for x in near]
    window = []
    for x in near + far:
        window += [x] + [ahead(x, "depth", d) for d in cores]

    source, target = scores_of(features, w_value, att_src, att_dst)
    link = links_of(tile_cols, tile_count, neighbours, tile)
    near_targets = [target] + [ahead(target, AXES, k * depths) for k in range(1, cols)]
    near_targets = jnp.stack(near_targets)
    targets = []
    for t in (near_targets, ahead(near_targets, "row", 1)):
        targets += [t] + [ahead(t, "depth", d) for d in cores]

    coef = coefs_of(chips, depths, tile_cols, tile_count, source, link, *targets)
    gathered = early_of(chips, depths, depths, tile_cols, tile_count, coef, *window[:-depths])
    return late_of(chips, depths, tile_cols, tile_count, gathered, coef, w_value, *window[-depths:])


def solution(mesh):
    placed = (
        P(AXES, None),
        P(),
        P(),
        P(),
        P("row", None),
        P("row"),
        P("row", None),
    )

    return jax.shard_map(
        on_device,
        mesh=mesh,
        in_specs=placed,
        out_specs=P(AXES, None),
        check_vma=False,
    )
```

profile of v0, /device:TPU:25, one launch (start us, length us, event | category | flops | bytes accessed | tf_op | source)
XLA Modules:
  0.0 67.9 jit_solution(13923059980464305429)
XLA Ops:
  0.0 2.3 %copy-done = bf16[768,3072]{1,0:T(8,128)(2,1)S(1)} copy-done((bf16[768,3072]{1,0:T(8,128)(2,1)S(1)}, bf16[768,3072]{1,0:T(8,128)(2,1)}, u32[]{:S(2)}) %copy-start) | copy-done | bytes 4718616
  2.3 0.9 %copy-done.2 = bf16[128,768]{1,0:T(8,128)(2,1)S(1)} copy-done((bf16[128,768]{1,0:T(8,128)(2,1)S(1)}, bf16[128,768]{1,0:T(8,128)(2,1)}, u32[]{:S(2)}) %copy-start.2) | copy-done | bytes 196632
  3.3 0.7 %copy-done.12 = bf16[4,768]{1,0:T(4,128)(2,1)S(1)} copy-done((bf16[4,768]{1,0:T(4,128)(2,1)S(1)}, bf16[4,768]{1,0:T(4,128)(2,1)}, u32[]{:S(2)}) %copy-start.12) | copy-done | bytes 6168
  4.0 0.7 %copy-done.13 = bf16[4,768]{1,0:T(4,128)(2,1)S(1)} copy-done((bf16[4,768]{1,0:T(4,128)(2,1)S(1)}, bf16[4,768]{1,0:T(4,128)(2,1)}, u32[]{:S(2)}) %copy-start.13) | copy-done | bytes 6168
  4.7 1.5 %scores.1 = (f32[128,4]{1,0:T(8,128)S(1)}, f32[4,128]{1,0:T(4,128)S(1)}) custom-call(bf16[128,768]{1,0:T(8,128)(2,1)S(1)} %copy-done.2, bf16[768,3072]{1,0:T(8,128)(2,1)S(1)} %copy-done, bf16[4,768]{1,0:T(4,128)(2,1)S(1)} %copy-done.12, bf16[4,768]{1,0:T(4,128)(2,1)S(1)} %copy-done.13), custom_call_target="tpu_custom_call" | custom-call | flops 603979776 | bytes 4718592 | tf_op jit(solution)/shard_map/scores/pallas_call | solution.py:177
  6.4 5.0 %collective-permute-start.2 = (f32[4,128]{1,0:T(4,128)S(1)}, f32[4,128]{1,0:T(4,128)S(1)}, u32[]{:S(2)}, u32[]{:S(2)}) collective-permute-start(f32[4,128]{1,0:T(4,128)S(1)} %get-tuple-element.8), channel_id=1, source_target_pairs={{6,0},{7,1},{8,2},{9,3},{10,4},{11,5},{12,6},{13,7},{14,8},{15,9},... | collective-permute-start | bytes 6152 | tf_op jit(solution)/shard_map/ppermute | solution.py:24
  11.7 1.2 %collective-permute-start.9 = (bf16[128,768]{1,0:T(8,128)(2,1)S(1)}, bf16[128,768]{1,0:T(8,128)(2,1)S(1)}, u32[]{:S(2)}, u32[]{:S(2)}) collective-permute-start(bf16[128,768]{1,0:T(8,128)(2,1)S(1)} %copy-done.2), channel_id=1, source_target_pairs={{4,0},{5,1},{6,2},{7,3},{8,4},{9,5},{10,6},{11,7},{12,8},{13,9},{1... | collective-permute-start | bytes 589832 | tf_op jit(solution)/shard_map/ppermute | solution.py:24
  12.8 3.2 %collective-permute-start.11 = (bf16[128,768]{1,0:T(8,128)(2,1)S(1)}, bf16[128,768]{1,0:T(8,128)(2,1)S(1)}, u32[]{:S(2)}, u32[]{:S(2)}) collective-permute-start(bf16[128,768]{1,0:T(8,128)(2,1)S(1)} %copy-done.2), channel_id=1, source_target_pairs={{6,0},{7,1},{8,2},{9,3},{10,4},{11,5},{12,6},{13,7},{14,8},{15,9},... | collective-permute-start | bytes 589832 | tf_op jit(solution)/shard_map/ppermute | solution.py:24
  16.3 2.2 %collective-permute-start.4 = (f32[4,4,128]{2,1,0:T(4,128)S(1)}, f32[4,4,128]{2,1,0:T(4,128)S(1)}, u32[]{:S(2)}, u32[]{:S(2)}) collective-permute-start(f32[4,4,128]{2,1,0:T(4,128)S(1)} %pad_maximum_fusion.refs_0_), channel_id=1, source_target_pairs={{8,0},{16,8},{24,16},{0,24},{9,1},{17,9},{25,17},{1,25},{10,2},{18... | collective-permute-start | bytes 24584 | tf_op jit(solution)/shard_map/ppermute | solution.py:24
  18.5 14.6 %collective-permute-done.4.refs_2_ = f32[4,4,128]{2,1,0:T(4,128)S(1)} collective-permute-done((f32[4,4,128]{2,1,0:T(4,128)S(1)}, f32[4,4,128]{2,1,0:T(4,128)S(1)}, u32[]{:S(2)}, u32[]{:S(2)}) %collective-permute-start.4) | collective-permute-done | bytes 8224 | tf_op jit(solution)/shard_map/ppermute | solution.py:24
  33.6 0.8 %collective-permute-done.3.refs_1_ = f32[4,4,128]{2,1,0:T(4,128)S(1)} collective-permute-done((f32[4,4,128]{2,1,0:T(4,128)S(1)}, f32[4,4,128]{2,1,0:T(4,128)S(1)}, u32[]{:S(2)}, u32[]{:S(2)}) %collective-permute-start.3) | collective-permute-done | bytes 8224 | tf_op jit(solution)/shard_map/ppermute | solution.py:24
  34.4 0.6 copy-done.7
  35.4 0.6 copy-done.5
  36.2 0.6 copy-done.9
  37.1 1.2 %collective-permute-start.15 = (bf16[128,768]{1,0:T(8,128)(2,1)S(1)}, bf16[128,768]{1,0:T(8,128)(2,1)S(1)}, u32[]{:S(2)}, u32[]{:S(2)}) collective-permute-start(bf16[128,768]{1,0:T(8,128)(2,1)S(1)} %collective-permute-done.7.refs_2_), channel_id=1, source_target_pairs={{8,0},{16,8},{24,16},{0,24},{9,1},{17,9},{25,17},{1,25},{10,2},{18... | collective-permute-start | bytes 589832 | tf_op jit(solution)/shard_map/ppermute | solution.py:24
  38.6 0.7 %collective-permute-start.10 = (bf16[128,768]{1,0:T(8,128)(2,1)S(1)}, bf16[128,768]{1,0:T(8,128)(2,1)S(1)}, u32[]{:S(2)}, u32[]{:S(2)}) collective-permute-start(bf16[128,768]{1,0:T(8,128)(2,1)S(1)} %collective-permute-done.9.refs_4_), channel_id=1, source_target_pairs={{1,0},{0,1},{3,2},{2,3},{5,4},{4,5},{7,6},{6,7},{9,8},{8,9},{11,10... | collective-permute-start | bytes 589832 | tf_op jit(solution)/shard_map/ppermute | solution.py:24
  39.4 1.2 %collective-permute-start.19 = (bf16[128,768]{1,0:T(8,128)(2,1)S(1)}, bf16[128,768]{1,0:T(8,128)(2,1)S(1)}, u32[]{:S(2)}, u32[]{:S(2)}) collective-permute-start(bf16[128,768]{1,0:T(8,128)(2,1)S(1)} %collective-permute-done.11.refs_6_), channel_id=1, source_target_pairs={{8,0},{16,8},{24,16},{0,24},{9,1},{17,9},{25,17},{1,25},{10,2},{18... | collective-permute-start | bytes 589832 | tf_op jit(solution)/shard_map/ppermute | solution.py:24
  40.5 2.9 %collective-permute-done.15.refs_10_ = bf16[128,768]{1,0:T(8,128)(2,1)S(1)} collective-permute-done((bf16[128,768]{1,0:T(8,128)(2,1)S(1)}, bf16[128,768]{1,0:T(8,128)(2,1)S(1)}, u32[]{:S(2)}, u32[]{:S(2)}) %collective-permute-start.15) | collective-permute-done | bytes 196640 | tf_op jit(solution)/shard_map/ppermute | solution.py:24
  43.4 1.7 %collective-permute-start.8 = (bf16[128,768]{1,0:T(8,128)(2,1)S(1)}, bf16[128,768]{1,0:T(8,128)(2,1)S(1)}, u32[]{:S(2)}, u32[]{:S(2)}) collective-permute-start(bf16[128,768]{1,0:T(8,128)(2,1)S(1)} %collective-permute-done.7.refs_2_), channel_id=1, source_target_pairs={{1,0},{0,1},{3,2},{2,3},{5,4},{4,5},{7,6},{6,7},{9,8},{8,9},{11,10... | collective-permute-start | bytes 589832 | tf_op jit(solution)/shard_map/ppermute | solution.py:24
  45.1 2.6 %collective-permute-done.17.refs_12_ = bf16[128,768]{1,0:T(8,128)(2,1)S(1)} collective-permute-done((bf16[128,768]{1,0:T(8,128)(2,1)S(1)}, bf16[128,768]{1,0:T(8,128)(2,1)S(1)}, u32[]{:S(2)}, u32[]{:S(2)}) %collective-permute-start.17) | collective-permute-done | bytes 196640 | tf_op jit(solution)/shard_map/ppermute | solution.py:24
  47.7 1.7 %collective-permute-start.14 = (bf16[128,768]{1,0:T(8,128)(2,1)S(1)}, bf16[128,768]{1,0:T(8,128)(2,1)S(1)}, u32[]{:S(2)}, u32[]{:S(2)}) collective-permute-start(bf16[128,768]{1,0:T(8,128)(2,1)S(1)} %collective-permute-done.13.refs_8_), channel_id=1, source_target_pairs={{1,0},{0,1},{3,2},{2,3},{5,4},{4,5},{7,6},{6,7},{9,8},{8,9},{11,10... | collective-permute-start | bytes 589832 | tf_op jit(solution)/shard_map/ppermute | solution.py:24
  49.3 0.5 collective-permute-start.18
  49.8 2.0 %collective-permute-done.19.refs_0_ = bf16[128,768]{1,0:T(8,128)(2,1)S(1)} collective-permute-done((bf16[128,768]{1,0:T(8,128)(2,1)S(1)}, bf16[128,768]{1,0:T(8,128)(2,1)S(1)}, u32[]{:S(2)}, u32[]{:S(2)}) %collective-permute-start.19) | collective-permute-done | bytes 196640 | tf_op jit(solution)/shard_map/ppermute | solution.py:24
  51.9 1.0 %collective-permute-start.20 = (bf16[128,768]{1,0:T(8,128)(2,1)S(1)}, bf16[128,768]{1,0:T(8,128)(2,1)}, u32[]{:S(2)}, u32[]{:S(2)}) collective-permute-start(bf16[128,768]{1,0:T(8,128)(2,1)S(1)} %collective-permute-done.19.refs_0_), channel_id=1, source_target_pairs={{1,0},{0,1},{3,2},{2,3},{5,4},{4,5},{7,6},{6,7},{9,8},{8,9},{11,10... | collective-permute-start | bytes 589832 | tf_op jit(solution)/shard_map/ppermute | solution.py:24
  52.9 1.0 %copy.8.near_ref = s32[1024,16]{1,0:T(8,128)S(1)} copy(s32[1024,16]{0,1:T(8,128)} %param.13) | data formatting | bytes 131072 | tf_op args[6]
  54.0 1.4 %links.1.link_ref = s32[128,128]{1,0:T(8,128)S(1)} custom-call(s32[8,8]{1,0:T(8,128)S(1)} %copy-done.4, s32[8]{0:T(128)S(1)} %copy-done.11, s32[1024,16]{1,0:T(8,128)S(1)} %copy.8.near_ref), custom_call_target="tpu_custom_call" | custom-call | flops 2097152 | bytes 65536 | tf_op jit(solution)/shard_map/links/pallas_call | solution.py:194
  55.4 0.7 %copy-done.6 = f32[4,4,128]{2,1,0:T(4,128)S(1)} copy-done((f32[4,4,128]{2,1,0:T(4,128)S(1)}, f32[4,4,128]{2,1,0:T(4,128)}, u32[]{:S(2)}) %copy-start.6) | copy-done | bytes 8216
  56.1 0.7 %copy-done.8 = f32[4,4,128]{2,1,0:T(4,128)S(1)} copy-done((f32[4,4,128]{2,1,0:T(4,128)S(1)}, f32[4,4,128]{2,1,0:T(4,128)}, u32[]{:S(2)}) %copy-start.8) | copy-done | bytes 8216
  56.8 0.7 %copy-done.10 = f32[4,4,128]{2,1,0:T(4,128)S(1)} copy-done((f32[4,4,128]{2,1,0:T(4,128)S(1)}, f32[4,4,128]{2,1,0:T(4,128)}, u32[]{:S(2)}) %copy-start.10) | copy-done | bytes 8216
  57.5 3.0 %coef.1.coef_ref = bf16[512,1024]{1,0:T(8,128)(2,1)S(1)} custom-call(s32[8,8]{1,0:T(8,128)S(1)} %copy-done.4, s32[8]{0:T(128)S(1)} %copy-done.11, f32[128,4]{1,0:T(8,128)S(1)} %get-tuple-element.7.source_ref, s32[128,128]{1,0:T(8,128)S(1)} %links.1.link_ref, f32[4,4,128]{2,1,0:T(4,128)S(1)} %pad_maximum_fusion.refs_0_, f32[4,4,128]{2,1,0:T(4,128)S(1)} %copy-done.8, ...), custom_call_target="tpu_custom_call" | custom-call | flops 4194304 | bytes 2097152 | tf_op jit(solution)/shard_map/coef/pallas_call | solution.py:218
  60.5 4.3 %early.1.gathered_ref = f32[512,768]{1,0:T(8,128)S(1)} custom-call(s32[8,8]{1,0:T(8,128)S(1)} %copy-done.4, s32[8]{0:T(128)S(1)} %copy-done.11, bf16[512,1024]{1,0:T(8,128)(2,1)S(1)} %coef.1.coef_ref, bf16[128,768]{1,0:T(8,128)(2,1)S(1)} %copy-done.3, bf16[128,768]{1,0:T(8,128)(2,1)S(1)} %collective-permute-done.6.refs_1_, ...), custom_call_target="tpu_custom_call" | custom-call | flops 805306368 | bytes 3145728 | tf_op jit(solution)/shard_map/early/pallas_call | solution.py:237
  64.9 3.0 %late.1 = bf16[128,768]{1,0:T(8,128)(2,1)} custom-call(s32[8,8]{1,0:T(8,128)S(1)} %copy-done.4, s32[8]{0:T(128)S(1)} %copy-done.11, f32[512,768]{1,0:T(8,128)S(1)} %early.1.gathered_ref, bf16[512,1024]{1,0:T(8,128)(2,1)S(1)} %coef.1.coef_ref, bf16[768,3072]{1,0:T(8,128)(2,1)S(1)} %copy-done.1, bf16[128,768]{1,0:T(8,128)(2,1)S(1)} %collective-permute-done.19.refs_0_, ...), custom_call_target="tpu_custom_call" | custom-call | flops 603979776 | bytes 1572864 | tf_op jit(solution)/shard_map/late/pallas_call | solution.py:253
  (45 shorter events, 2.6 us)
Async XLA Ops:
  0.0 2.3 %copy-start = (bf16[768,3072]{1,0:T(8,128)(2,1)S(1)}, bf16[768,3072]{1,0:T(8,128)(2,1)}, u32[]{:S(2)}) copy-start(bf16[768,3072]{1,0:T(8,128)(2,1)} %w_ref.3) | copy-start | bytes 14155780
  2.3 0.9 %copy-start.2 = (bf16[128,768]{1,0:T(8,128)(2,1)S(1)}, bf16[128,768]{1,0:T(8,128)(2,1)}, u32[]{:S(2)}) copy-start(bf16[128,768]{1,0:T(8,128)(2,1)} %refs_0_.1) | copy-start | bytes 589828
  3.3 0.7 %copy-start.12 = (bf16[4,768]{1,0:T(4,128)(2,1)S(1)}, bf16[4,768]{1,0:T(4,128)(2,1)}, u32[]{:S(2)}) copy-start(bf16[4,768]{1,0:T(4,128)(2,1)} %src_ref.1) | copy-start | bytes 18436
  4.0 0.7 %copy-start.13 = (bf16[4,768]{1,0:T(4,128)(2,1)S(1)}, bf16[4,768]{1,0:T(4,128)(2,1)}, u32[]{:S(2)}) copy-start(bf16[4,768]{1,0:T(4,128)(2,1)} %dst_ref.1) | copy-start | bytes 18436
  4.6 49.3 %copy-start.4 = (s32[8,8]{1,0:T(8,128)S(1)}, s32[8,8]{1,0:T(8,128)}, u32[]{:S(2)}) copy-start(s32[8,8]{1,0:T(8,128)} %cols_ref.7) | copy-start | bytes 772
  4.7 49.3 %copy-start.11 = (s32[8]{0:T(128)S(1)}, s32[8]{0:T(128)}, u32[]{:S(2)}) copy-start(s32[8]{0:T(128)} %count_ref.7) | copy-start | bytes 100
  4.7 55.9 %copy-start.3 = (bf16[128,768]{1,0:T(8,128)(2,1)S(1)}, bf16[128,768]{1,0:T(8,128)(2,1)}, u32[]{:S(2)}) copy-start(bf16[128,768]{1,0:T(8,128)(2,1)} %refs_0_.1) | copy-start | bytes 589828
  6.2 6.6 %collective-permute-start = (f32[4,128]{1,0:T(4,128)S(1)}, f32[4,128]{1,0:T(4,128)S(1)}, u32[]{:S(2)}, u32[]{:S(2)}) collective-permute-start(f32[4,128]{1,0:T(4,128)S(1)} %get-tuple-element.8), channel_id=1, source_target_pairs={{2,0},{3,1},{4,2},{5,3},{6,4},{7,5},{8,6},{9,7},{10,8},{11,9},{12,... | collective-permute-start | bytes 6152 | tf_op jit(solution)/shard_map/ppermute | solution.py:24
  6.4 9.7 %collective-permute-start.1 = (f32[4,128]{1,0:T(4,128)S(1)}, f32[4,128]{1,0:T(4,128)S(1)}, u32[]{:S(2)}, u32[]{:S(2)}) collective-permute-start(f32[4,128]{1,0:T(4,128)S(1)} %get-tuple-element.8), channel_id=1, source_target_pairs={{4,0},{5,1},{6,2},{7,3},{8,4},{9,5},{10,6},{11,7},{12,8},{13,9},{1... | collective-permute-start | bytes 6152 | tf_op jit(solution)/shard_map/ppermute | solution.py:24
  6.4 9.9 %collective-permute-start.2 = (f32[4,128]{1,0:T(4,128)S(1)}, f32[4,128]{1,0:T(4,128)S(1)}, u32[]{:S(2)}, u32[]{:S(2)}) collective-permute-start(f32[4,128]{1,0:T(4,128)S(1)} %get-tuple-element.8), channel_id=1, source_target_pairs={{6,0},{7,1},{8,2},{9,3},{10,4},{11,5},{12,6},{13,7},{14,8},{15,9},... | collective-permute-start | bytes 6152 | tf_op jit(solution)/shard_map/ppermute | solution.py:24
  11.4 25.8 %collective-permute-start.7 = (bf16[128,768]{1,0:T(8,128)(2,1)S(1)}, bf16[128,768]{1,0:T(8,128)(2,1)S(1)}, u32[]{:S(2)}, u32[]{:S(2)}) collective-permute-start(bf16[128,768]{1,0:T(8,128)(2,1)S(1)} %copy-done.2), channel_id=1, source_target_pairs={{2,0},{3,1},{4,2},{5,3},{6,4},{7,5},{8,6},{9,7},{10,8},{11,9},{12,... | collective-permute-start | bytes 589832 | tf_op jit(solution)/shard_map/ppermute | solution.py:24
  11.7 26.7 %collective-permute-start.9 = (bf16[128,768]{1,0:T(8,128)(2,1)S(1)}, bf16[128,768]{1,0:T(8,128)(2,1)S(1)}, u32[]{:S(2)}, u32[]{:S(2)}) collective-permute-start(bf16[128,768]{1,0:T(8,128)(2,1)S(1)} %copy-done.2), channel_id=1, source_target_pairs={{4,0},{5,1},{6,2},{7,3},{8,4},{9,5},{10,6},{11,7},{12,8},{13,9},{1... | collective-permute-start | bytes 589832 | tf_op jit(solution)/shard_map/ppermute | solution.py:24
  12.8 25.8 %collective-permute-start.11 = (bf16[128,768]{1,0:T(8,128)(2,1)S(1)}, bf16[128,768]{1,0:T(8,128)(2,1)S(1)}, u32[]{:S(2)}, u32[]{:S(2)}) collective-permute-start(bf16[128,768]{1,0:T(8,128)(2,1)S(1)} %copy-done.2), channel_id=1, source_target_pairs={{6,0},{7,1},{8,2},{9,3},{10,4},{11,5},{12,6},{13,7},{14,8},{15,9},... | collective-permute-start | bytes 589832 | tf_op jit(solution)/shard_map/ppermute | solution.py:24
  16.0 23.2 %collective-permute-start.13 = (bf16[128,768]{1,0:T(8,128)(2,1)S(1)}, bf16[128,768]{1,0:T(8,128)(2,1)S(1)}, u32[]{:S(2)}, u32[]{:S(2)}) collective-permute-start(bf16[128,768]{1,0:T(8,128)(2,1)S(1)} %copy-done.2), channel_id=1, source_target_pairs={{8,0},{16,8},{24,16},{0,24},{9,1},{17,9},{25,17},{1,25},{10,2},{18... | collective-permute-start | bytes 589832 | tf_op jit(solution)/shard_map/ppermute | solution.py:24
  16.3 16.8 %collective-permute-start.4 = (f32[4,4,128]{2,1,0:T(4,128)S(1)}, f32[4,4,128]{2,1,0:T(4,128)S(1)}, u32[]{:S(2)}, u32[]{:S(2)}) collective-permute-start(f32[4,4,128]{2,1,0:T(4,128)S(1)} %pad_maximum_fusion.refs_0_), channel_id=1, source_target_pairs={{8,0},{16,8},{24,16},{0,24},{9,1},{17,9},{25,17},{1,25},{10,2},{18... | collective-permute-start | bytes 24584 | tf_op jit(solution)/shard_map/ppermute | solution.py:24
  33.1 1.3 %collective-permute-start.3 = (f32[4,4,128]{2,1,0:T(4,128)S(1)}, f32[4,4,128]{2,1,0:T(4,128)S(1)}, u32[]{:S(2)}, u32[]{:S(2)}) collective-permute-start(f32[4,4,128]{2,1,0:T(4,128)S(1)} %pad_maximum_fusion.refs_0_), channel_id=1, source_target_pairs={{1,0},{0,1},{3,2},{2,3},{5,4},{4,5},{7,6},{6,7},{9,8},{8,9},{11,10... | collective-permute-start | bytes 24584 | tf_op jit(solution)/shard_map/ppermute | solution.py:24
  35.0 1.2 %collective-permute-start.5 = (f32[4,4,128]{2,1,0:T(4,128)S(1)}, f32[4,4,128]{2,1,0:T(4,128)S(1)}, u32[]{:S(2)}, u32[]{:S(2)}) collective-permute-start(f32[4,4,128]{2,1,0:T(4,128)S(1)} %collective-permute-done.4.refs_2_), channel_id=1, source_target_pairs={{1,0},{0,1},{3,2},{2,3},{5,4},{4,5},{7,6},{6,7},{9,8},{8,9},{11,10... | collective-permute-start | bytes 24584 | tf_op jit(solution)/shard_map/ppermute | solution.py:24
  36.8 2.6 %collective-permute-start.6 = (bf16[128,768]{1,0:T(8,128)(2,1)S(1)}, bf16[128,768]{1,0:T(8,128)(2,1)S(1)}, u32[]{:S(2)}, u32[]{:S(2)}) collective-permute-start(bf16[128,768]{1,0:T(8,128)(2,1)S(1)} %copy-done.2), channel_id=1, source_target_pairs={{1,0},{0,1},{3,2},{2,3},{5,4},{4,5},{7,6},{6,7},{9,8},{8,9},{11,10... | collective-permute-start | bytes 589832 | tf_op jit(solution)/shard_map/ppermute | solution.py:24
  37.1 6.3 %collective-permute-start.15 = (bf16[128,768]{1,0:T(8,128)(2,1)S(1)}, bf16[128,768]{1,0:T(8,128)(2,1)S(1)}, u32[]{:S(2)}, u32[]{:S(2)}) collective-permute-start(bf16[128,768]{1,0:T(8,128)(2,1)S(1)} %collective-permute-done.7.refs_2_), channel_id=1, source_target_pairs={{8,0},{16,8},{24,16},{0,24},{9,1},{17,9},{25,17},{1,25},{10,2},{18... | collective-permute-start | bytes 589832 | tf_op jit(solution)/shard_map/ppermute | solution.py:24
  38.3 9.3 %collective-permute-start.17 = (bf16[128,768]{1,0:T(8,128)(2,1)S(1)}, bf16[128,768]{1,0:T(8,128)(2,1)S(1)}, u32[]{:S(2)}, u32[]{:S(2)}) collective-permute-start(bf16[128,768]{1,0:T(8,128)(2,1)S(1)} %collective-permute-done.9.refs_4_), channel_id=1, source_target_pairs={{8,0},{16,8},{24,16},{0,24},{9,1},{17,9},{25,17},{1,25},{10,2},{18... | collective-permute-start | bytes 589832 | tf_op jit(solution)/shard_map/ppermute | solution.py:24
  38.6 10.7 %collective-permute-start.10 = (bf16[128,768]{1,0:T(8,128)(2,1)S(1)}, bf16[128,768]{1,0:T(8,128)(2,1)S(1)}, u32[]{:S(2)}, u32[]{:S(2)}) collective-permute-start(bf16[128,768]{1,0:T(8,128)(2,1)S(1)} %collective-permute-done.9.refs_4_), channel_id=1, source_target_pairs={{1,0},{0,1},{3,2},{2,3},{5,4},{4,5},{7,6},{6,7},{9,8},{8,9},{11,10... | collective-permute-start | bytes 589832 | tf_op jit(solution)/shard_map/ppermute | solution.py:24
  39.3 10.0 %collective-permute-start.12 = (bf16[128,768]{1,0:T(8,128)(2,1)S(1)}, bf16[128,768]{1,0:T(8,128)(2,1)S(1)}, u32[]{:S(2)}, u32[]{:S(2)}) collective-permute-start(bf16[128,768]{1,0:T(8,128)(2,1)S(1)} %collective-permute-done.11.refs_6_), channel_id=1, source_target_pairs={{1,0},{0,1},{3,2},{2,3},{5,4},{4,5},{7,6},{6,7},{9,8},{8,9},{11,10... | collective-permute-start | bytes 589832 | tf_op jit(solution)/shard_map/ppermute | solution.py:24
  39.4 12.5 %collective-permute-start.19 = (bf16[128,768]{1,0:T(8,128)(2,1)S(1)}, bf16[128,768]{1,0:T(8,128)(2,1)S(1)}, u32[]{:S(2)}, u32[]{:S(2)}) collective-permute-start(bf16[128,768]{1,0:T(8,128)(2,1)S(1)} %collective-permute-done.11.refs_6_), channel_id=1, source_target_pairs={{8,0},{16,8},{24,16},{0,24},{9,1},{17,9},{25,17},{1,25},{10,2},{18... | collective-permute-start | bytes 589832 | tf_op jit(solution)/shard_map/ppermute | solution.py:24
  43.4 17.0 %collective-permute-start.8 = (bf16[128,768]{1,0:T(8,128)(2,1)S(1)}, bf16[128,768]{1,0:T(8,128)(2,1)S(1)}, u32[]{:S(2)}, u32[]{:S(2)}) collective-permute-start(bf16[128,768]{1,0:T(8,128)(2,1)S(1)} %collective-permute-done.7.refs_2_), channel_id=1, source_target_pairs={{1,0},{0,1},{3,2},{2,3},{5,4},{4,5},{7,6},{6,7},{9,8},{8,9},{11,10... | collective-permute-start | bytes 589832 | tf_op jit(solution)/shard_map/ppermute | solution.py:24
  47.7 12.8 %collective-permute-start.14 = (bf16[128,768]{1,0:T(8,128)(2,1)S(1)}, bf16[128,768]{1,0:T(8,128)(2,1)S(1)}, u32[]{:S(2)}, u32[]{:S(2)}) collective-permute-start(bf16[128,768]{1,0:T(8,128)(2,1)S(1)} %collective-permute-done.13.refs_8_), channel_id=1, source_target_pairs={{1,0},{0,1},{3,2},{2,3},{5,4},{4,5},{7,6},{6,7},{9,8},{8,9},{11,10... | collective-permute-start | bytes 589832 | tf_op jit(solution)/shard_map/ppermute | solution.py:24
  49.3 11.2 %collective-permute-start.16 = (bf16[128,768]{1,0:T(8,128)(2,1)S(1)}, bf16[128,768]{1,0:T(8,128)(2,1)S(1)}, u32[]{:S(2)}, u32[]{:S(2)}) collective-permute-start(bf16[128,768]{1,0:T(8,128)(2,1)S(1)} %collective-permute-done.15.refs_10_), channel_id=1, source_target_pairs={{1,0},{0,1},{3,2},{2,3},{5,4},{4,5},{7,6},{6,7},{9,8},{8,9},{11,10... | collective-permute-start | bytes 589832 | tf_op jit(solution)/shard_map/ppermute | solution.py:24
  49.3 11.2 %collective-permute-start.18 = (bf16[128,768]{1,0:T(8,128)(2,1)S(1)}, bf16[128,768]{1,0:T(8,128)(2,1)S(1)}, u32[]{:S(2)}, u32[]{:S(2)}) collective-permute-start(bf16[128,768]{1,0:T(8,128)(2,1)S(1)} %collective-permute-done.17.refs_12_), channel_id=1, source_target_pairs={{1,0},{0,1},{3,2},{2,3},{5,4},{4,5},{7,6},{6,7},{9,8},{8,9},{11,10... | collective-permute-start | bytes 589832 | tf_op jit(solution)/shard_map/ppermute | solution.py:24
  51.9 13.0 %collective-permute-start.20 = (bf16[128,768]{1,0:T(8,128)(2,1)S(1)}, bf16[128,768]{1,0:T(8,128)(2,1)}, u32[]{:S(2)}, u32[]{:S(2)}) collective-permute-start(bf16[128,768]{1,0:T(8,128)(2,1)S(1)} %collective-permute-done.19.refs_0_), channel_id=1, source_target_pairs={{1,0},{0,1},{3,2},{2,3},{5,4},{4,5},{7,6},{6,7},{9,8},{8,9},{11,10... | collective-permute-start | bytes 589832 | tf_op jit(solution)/shard_map/ppermute | solution.py:24
  54.0 10.9 %copy-start.1 = (bf16[768,3072]{1,0:T(8,128)(2,1)S(1)}, bf16[768,3072]{1,0:T(8,128)(2,1)}, u32[]{:S(2)}) copy-start(bf16[768,3072]{1,0:T(8,128)(2,1)} %w_ref.3) | copy-start | bytes 14155780
  55.4 0.7 %copy-start.6 = (f32[4,4,128]{2,1,0:T(4,128)S(1)}, f32[4,4,128]{2,1,0:T(4,128)}, u32[]{:S(2)}) copy-start(f32[4,4,128]{2,1,0:T(4,128)} %copy-done.5) | copy-start | bytes 24580
  56.1 0.7 %copy-start.8 = (f32[4,4,128]{2,1,0:T(4,128)S(1)}, f32[4,4,128]{2,1,0:T(4,128)}, u32[]{:S(2)}) copy-start(f32[4,4,128]{2,1,0:T(4,128)} %copy-done.7) | copy-start | bytes 24580
  56.8 0.7 %copy-start.10 = (f32[4,4,128]{2,1,0:T(4,128)S(1)}, f32[4,4,128]{2,1,0:T(4,128)}, u32[]{:S(2)}) copy-start(f32[4,4,128]{2,1,0:T(4,128)} %copy-done.9) | copy-start | bytes 24580
  (3 other events, 1.8 us)
where the time goes:
time: 68.3 us; the launch traced here: 67.9 us
  waiting for transfers between devices  23.2 us (34%)
  starting transfers between devices  21.7 us (32%)
  Pallas kernels  13.2 us (19%)
  local copies, waits for them, and re-layouts  9.59 us (14%)
    ppermute x21, waiting for transfers between devices, ahead(): lax.ppermute(array, axis, [((i + by) % length, i) for i in range(length)])  23.2 us
    ppermute x21, starting transfers between devices, ahead(): lax.ppermute(array, axis, [((i + by) % length, i) for i in range(length)])  21.7 us
    unnamed x29, local copies, waits for them, and re-layouts  9.59 us
    pallas_call x1, Pallas kernels, early_of(): pl.pallas_call(functools.partial(early_kernel, chips, depths, late), out_...  4.34 us
    pallas_call x1, Pallas kernels, coefs_of(): pl.pallas_call(functools.partial(coef_kernel, chips, depths), out_shape=j...  2.99 us
    pallas_call x1, Pallas kernels, late_of(): pl.pallas_call(functools.partial(late_kernel, chips, depths), out_shape=j...  2.96 us
    pallas_call x1, Pallas kernels, scores_of(): pl.pallas_call(score_kernel, out_shape=(jax.ShapeDtypeStruct((rows, heads...  1.5 us
    pallas_call x1, Pallas kernels, links_of(): pl.pallas_call(link_kernel, out_shape=jax.ShapeDtypeStruct((tile, tile),...  1.39 us
  transfers between devices with their start and end apart: 21, of which 6 were waited for; matrix products, arithmetic and copies ran while one was open for 2% of the time, Pallas kernels for 13%

commit v1 on v0

v1 whole, which is shorter than its diff:
```python
import functools

import jax
import jax.numpy as jnp
from jax import lax
from jax.experimental import pallas as pl
from jax.experimental.pallas import tpu as pltpu
from jax.sharding import PartitionSpec as P


AXES = ("row", "col", "depth")
LEAK_SLOPE = 0.2
NEG_BIG = -1e30
VM = pl.BlockSpec(memory_space=pltpu.VMEM)
SM = pl.BlockSpec(memory_space=pltpu.SMEM)
HBM = pl.BlockSpec(memory_space=pltpu.HBM)
ANY = pl.BlockSpec(memory_space=pl.ANY)
F32 = jnp.float32
BF16 = jnp.bfloat16

EXTRA = 8

LAST = (((1,), (1,)), ((), ()))


def ahead(array, axis, by):
    length = lax.axis_size(axis)
    return lax.ppermute(array, axis, [((i + by) % length, i) for i in range(length)])


def place_of_device():
    depths = lax.axis_size("depth")
    chip = lax.axis_index("row") * lax.axis_size("col") + lax.axis_index("col")
    depth = lax.axis_index("depth")
    return chip, depth, lax.axis_index("col") * depths + depth


def window_tile(tile, chip, depth, chips, depths):
    step = tile // depths - chip
    step = jnp.where(step < 0, step + chips, step)
    side = tile % depths - depth
    side = jnp.where(side < 0, side + depths, side)
    return step * depths + side


def slot_tiles(cols_ref, count_ref, chips, depths):
    chip, depth, own = place_of_device()
    count = count_ref[own]
    return [
        jnp.where(s < count, window_tile(cols_ref[own, s], chip, depth, chips, depths), 0)
        for s in range(cols_ref.shape[1])
    ], count


def put_scores(message_ref, head, scores):
    rows = scores.shape[1]
    parts, rest = [], scores
    for _ in range(3):
        part = rest.astype(BF16).astype(F32)
        rest = rest - part
        parts.append(part)
    parts.append(jnp.zeros((EXTRA - 3, rows), F32))
    message_ref[rows:, head * rows : (head + 1) * rows] = jnp.concatenate(parts, axis=0).astype(BF16)


def score_kernel(features_ref, w_ref, src_ref, dst_ref, source_ref, message_ref, x, src, dst, w, sems):
    rows, _ = features_ref.shape
    heads, width = src_ref.shape
    small = [
        pltpu.make_async_copy(a, b, sems.at[heads + i])
        for i, (a, b) in enumerate(((features_ref, x), (src_ref, src), (dst_ref, dst)))
    ]
    copies = [
        pltpu.make_async_copy(w_ref.at[:, pl.ds(h * width, width)], w.at[h], sems.at[h])
        for h in range(heads)
    ]
    for copy in small + copies:
        copy.start()
    for copy in small:
        copy.wait()
    message_ref[:rows] = x[...]
    message_ref[rows:] = jnp.zeros((EXTRA, message_ref.shape[1]), BF16)
    for h in range(heads):
        copies[h].wait()
        value = jnp.dot(x[...], w[h], preferred_element_type=F32).astype(BF16)
        source = lax.dot_general(value, src[...], LAST, preferred_element_type=F32)
        target = lax.dot_general(dst[...], value, LAST, preferred_element_type=F32)
        source_ref[:, h : h + 1] = source[:, h : h + 1]
        put_scores(message_ref, h, target[h : h + 1, :])


def message_kernel(features_ref, w_ref, dst_ref, message_ref):
    rows, _ = features_ref.shape
    heads, width = dst_ref.shape
    message_ref[:rows] = features_ref[...]
    message_ref[rows:] = jnp.zeros((EXTRA, message_ref.shape[1]), BF16)
    for h in range(heads):
        value = jnp.dot(
            features_ref[...], w_ref[:, h * width : (h + 1) * width], preferred_element_type=F32
        ).astype(BF16)
        target = lax.dot_general(dst_ref[...], value, LAST, preferred_element_type=F32)
        put_scores(message_ref, h, target[h : h + 1, :])


def link_kernel(cols_ref, count_ref, near_ref, link_ref, near_scratch, sem):
    tile, near_count = near_scratch.shape
    _, _, own = place_of_device()
    copy = pltpu.make_async_copy(near_ref.at[pl.ds(own * tile, tile)], near_scratch, sem)
    copy.start()
    copy.wait()
    near = near_scratch[...]
    near_tile = near // tile
    bit = jnp.zeros(near.shape, jnp.int32)
    for s in range(cols_ref.shape[1]):
        listed = jnp.where(s < count_ref[own], cols_ref[own, s], -1)
        bit = jnp.where(near_tile == listed, 1 << s, bit)
    spot = near % tile
    lane = lax.broadcasted_iota(jnp.int32, (tile, tile), 1)
    row = lax.broadcasted_iota(jnp.int32, (tile, tile), 0)
    link = jnp.where(lane == row, 1, 0)
    for k in range(near_count):
        link = link | jnp.where(spot[:, k : k + 1] == lane, bit[:, k : k + 1], 0)
    link_ref[...] = link


def slot_of(window_place, places, listed):
    slot = -1
    for s, place in enumerate(places):
        slot = jnp.where((place == window_place) & listed[s], s, slot)
    return slot


def scores_in(extra, head, tile):
    parts = extra[:, head * tile : (head + 1) * tile].astype(F32)
    return parts[0:1] + parts[1:2] + parts[2:3]


def first_kernel(chips, depths, cols_ref, count_ref, source_ref, link_ref, *refs):
    message_refs, refs = refs[:-8], refs[-8:]
    peak_ref, total_ref, mixed_ref, picked, extras, targets, coef, sems = refs
    tile, heads = source_ref.shape
    places, count = slot_tiles(cols_ref, count_ref, chips, depths)
    slots = len(places)
    listed = [s < count for s in range(slots)]
    for w, ref in enumerate(message_refs):
        slot = slot_of(w, places, listed)

        @pl.when(slot >= 0)
        def _(ref=ref, slot=slot):
            pltpu.make_async_copy(
                ref.at[pl.ds(tile, EXTRA)], extras.at[slot], sems.at[0, slot]
            ).start()
            at = picked.at[pl.ds(pl.multiple_of(slot * tile, tile), tile)]
            pltpu.make_async_copy(ref.at[pl.ds(0, tile)], at, sems.at[1, slot]).start()

    held = 0
    copied = [listed[s] & (places[s] < len(message_refs)) for s in range(slots)]
    for s in range(slots):
        held = held + jnp.where(copied[s], 1 << s, 0)

        @pl.when(copied[s])
        def _(s=s):
            pltpu.make_async_copy(
                message_refs[0].at[pl.ds(tile, EXTRA)], extras.at[s], sems.at[0, s]
            ).wait()

        for h in range(heads):
            targets[h : h + 1, s * tile : (s + 1) * tile] = scores_in(extras[s], h, tile)

    block = 16

    def step(b, carry):
        at = pl.ds(pl.multiple_of(b * block, block), block)
        link = link_ref[at, :] & held
        linked = jnp.concatenate([link & (1 << s) for s in range(slots)], axis=1) != 0
        for h in range(heads):
            logits = source_ref[at, h : h + 1] + targets[h : h + 1, :]
            logits = jnp.where(linked, jnp.maximum(logits, LEAK_SLOPE * logits), NEG_BIG)
            peak = jnp.max(logits, axis=1, keepdims=True)
            weights = jnp.exp(logits - peak)
            peak_ref[at, h : h + 1] = peak
            total_ref[at, h : h + 1] = jnp.sum(weights, axis=1, keepdims=True)
            out = pl.ds(pl.multiple_of(h * tile + b * block, block), block)
            coef[out, :] = weights.astype(BF16)
        return carry

    lax.fori_loop(0, tile // block, step, 0)

    for s in range(slots):
        at = picked.at[pl.ds(s * tile, tile)]

        @pl.when(copied[s])
        def _(at=at, s=s):
            pltpu.make_async_copy(message_refs[0].at[pl.ds(0, tile)], at, sems.at[1, s]).wait()

        @pl.when(jnp.logical_not(copied[s]))
        def _(at=at):
            at[...] = jnp.zeros(at.shape, at.dtype)

    mixed_ref[...] = jnp.dot(coef[...], picked[...], preferred_element_type=F32)


def next_kernel(chips, depths, first, last, cols_ref, count_ref, source_ref, link_ref, *refs):
    tile, heads = source_ref.shape
    peak_in, total_in, mixed_in = refs[:3]
    if last:
        w_ref, message_refs = refs[3], refs[4:-3]
        out_ref, targets, coef = refs[-3:]
    else:
        message_refs = refs[3:-5]
        peak_ref, total_ref, mixed_ref, targets, coef = refs[-5:]
    width = mixed_in.shape[1]
    places, count = slot_tiles(cols_ref, count_ref, chips, depths)
    listed = [s < count for s in range(len(places))]
    bits = []
    for i, ref in enumerate(message_refs):
        slot = slot_of(first + i, places, listed)
        bits.append(jnp.where(slot >= 0, jnp.left_shift(1, jnp.maximum(slot, 0)), 0))
        for h in range(heads):
            targets[h : h + 1, i * tile : (i + 1) * tile] = scores_in(ref[tile:, :], h, tile)
    link = link_ref[...]
    linked = jnp.concatenate([link & bit for bit in bits], axis=1) != 0
    features = jnp.concatenate([ref[:tile, :] for ref in message_refs], axis=0)
    total = None
    for h in range(heads):
        logits = source_ref[:, h : h + 1] + targets[h : h + 1, :]
        logits = jnp.where(linked, jnp.maximum(logits, LEAK_SLOPE * logits), NEG_BIG)
        before = peak_in[:, h : h + 1]
        peak = jnp.maximum(before, jnp.max(logits, axis=1, keepdims=True))
        fade = jnp.exp(before - peak)
        weights = jnp.exp(logits - peak)
        weight = total_in[:, h : h + 1] * fade + jnp.sum(weights, axis=1, keepdims=True)
        weights = weights.astype(BF16)
        mixed = mixed_in[h * tile : (h + 1) * tile, :] * fade
        mixed = mixed + jnp.dot(weights, features, preferred_element_type=F32)
        if last:
            part = jnp.dot(
                (mixed * (1.0 / weight)).astype(BF16),
                w_ref[:, h * width : (h + 1) * width],
                preferred_element_type=F32,
            )
            total = part if total is None else total + part
        else:
            peak_ref[:, h : h + 1] = peak
            total_ref[:, h : h + 1] = weight
            mixed_ref[h * tile : (h + 1) * tile, :] = mixed
    if last:
        out = total * (1.0 / heads)
        out_ref[...] = jnp.where(out > 0, out, jnp.exp(out) - 1.0).astype(out_ref.dtype)


def scores_of(features, w_value, att_src, att_dst):
    (rows, width), heads = features.shape, att_src.shape[0]
    inputs = (features, w_value, att_src, att_dst)
    return pl.pallas_call(
        score_kernel,
        out_shape=(
            jax.ShapeDtypeStruct((rows, heads), F32),
            jax.ShapeDtypeStruct((rows + EXTRA, width), BF16),
        ),
        in_specs=[HBM] * 4,
        out_specs=(VM, VM),
        scratch_shapes=[
            pltpu.VMEM(features.shape, BF16),
            pltpu.VMEM(att_src.shape, BF16),
            pltpu.VMEM(att_dst.shape, BF16),
            pltpu.VMEM((heads, w_value.shape[0], att_src.shape[1]), BF16),
            pltpu.SemaphoreType.DMA((heads + 3,)),
        ],
        cost_estimate=pl.CostEstimate(
            flops=rows, bytes_accessed=rows, transcendentals=0
        ),
        compiler_params=pltpu.CompilerParams(vmem_limit_bytes=16 << 20),
        name="scores",
    )(*[pltpu.with_memory_space_constraint(x, pltpu.HBM) for x in inputs])


def message_of(features, w_value, att_dst):
    (rows, width) = features.shape
    return pl.pallas_call(
        message_kernel,
        out_shape=jax.ShapeDtypeStruct((rows + EXTRA, width), BF16),
        in_specs=[VM] * 3,
        out_specs=VM,
        cost_estimate=pl.CostEstimate(
            flops=2 * rows * w_value.size, bytes_accessed=2 * w_value.size, transcendentals=0
        ),
        compiler_params=pltpu.CompilerParams(vmem_limit_bytes=8 << 20),
        name="message",
    )(features, w_value, att_dst)


def links_of(tile_cols, tile_count, neighbours, tile):
    return pl.pallas_call(
        link_kernel,
        out_shape=jax.ShapeDtypeStruct((tile, tile), jnp.int32),
        in_specs=[SM, SM, HBM],
        out_specs=VM,
        scratch_shapes=[
            pltpu.VMEM((tile, neighbours.shape[1]), jnp.int32),
            pltpu.SemaphoreType.DMA,
        ],
        cost_estimate=pl.CostEstimate(
            flops=tile, bytes_accessed=tile, transcendentals=0
        ),
        compiler_params=pltpu.CompilerParams(vmem_limit_bytes=4 << 20),
        name="links",
    )(tile_cols, tile_count, neighbours)


def stats_shape(tile, heads, width):
    return (
        jax.ShapeDtypeStruct((tile, heads), F32),
        jax.ShapeDtypeStruct((tile, heads), F32),
        jax.ShapeDtypeStruct((heads * tile, width), F32),
    )


def first_of(chips, depths, tile_cols, tile_count, source, link, *messages):
    tile, heads = source.shape
    width = messages[0].shape[1]
    slots = tile_cols.shape[1]
    return pl.pallas_call(
        functools.partial(first_kernel, chips, depths),
        out_shape=stats_shape(tile, heads, width),
        in_specs=[SM, SM, VM, VM] + [ANY] * len(messages),
        out_specs=(VM,) * 3,
        scratch_shapes=[
            pltpu.VMEM((slots * tile, width), BF16),
            pltpu.VMEM((slots, EXTRA, width), BF16),
            pltpu.VMEM((heads, slots * tile), F32),
            pltpu.VMEM((heads * tile, slots * tile), BF16),
            pltpu.SemaphoreType.DMA((2, slots)),
        ],
        cost_estimate=pl.CostEstimate(
            flops=2 * heads * tile * slots * tile * width,
            bytes_accessed=8 * heads * tile * width,
            transcendentals=heads * tile * slots * tile,
        ),
        compiler_params=pltpu.CompilerParams(vmem_limit_bytes=14 << 20),
        name="first",
    )(tile_cols, tile_count, source, link, *messages)


def next_of(chips, depths, first, tile_cols, tile_count, source, link, state, w_value, *messages):
    tile, heads = source.shape
    width = messages[0].shape[1]
    last = w_value is not None
    return pl.pallas_call(
        functools.partial(next_kernel, chips, depths, first, last),
        out_shape=jax.ShapeDtypeStruct((tile, width), BF16) if last else stats_shape(tile, heads, width),
        in_specs=[SM, SM] + [VM] * (5 + last + len(messages)),
        out_specs=VM if last else (VM,) * 3,
        scratch_shapes=[
            pltpu.VMEM((heads, len(messages) * tile), F32),
            pltpu.VMEM((heads * tile, len(messages) * tile), BF16),
        ],
        cost_estimate=pl.CostEstimate(
            flops=2 * heads * tile * tile * width * (len(messages) + 6 * last),
            bytes_accessed=8 * heads * tile * width,
            transcendentals=heads * tile * tile * len(messages),
        ),
        compiler_params=pltpu.CompilerParams(vmem_limit_bytes=14 << 20),
        name="final" if last else "middle",
    )(tile_cols, tile_count, source, link, *state, *((w_value,) if last else ()), *messages)


def on_device(features, w_value, att_src, att_dst, tile_cols, tile_count, neighbours):
    tile = features.shape[0]
    cols = lax.axis_size("col")
    depths = lax.axis_size("depth")
    chips = lax.axis_size("row") * cols
    cores = range(1, depths)

    source, message = scores_of(features, w_value, att_src, att_dst)
    link = links_of(tile_cols, tile_count, neighbours, tile)

    near = [message]
    for k in range(1, cols):
        arrived = ahead(features, AXES, k * depths)
        near.append(message_of(arrived, w_value, att_dst))
    far = [ahead(x, "row", 1) for x in near]
    window = []
    for x in near + far:
        window += [x] + [ahead(x, "depth", d) for d in cores]

    common = (tile_cols, tile_count, source, link)
    a, b = (cols + 1) * depths, len(window) - depths
    state = first_of(chips, depths, *common, *window[:a])
    state = next_of(chips, depths, a, *common, state, None, *window[a:b])
    return next_of(chips, depths, b, *common, state, w_value, *window[b:])


def solution(mesh):
    placed = (
        P(AXES, None),
        P(),
        P(),
        P(),
        P("row", None),
        P("row"),
        P("row", None),
    )

    return jax.shard_map(
        on_device,
        mesh=mesh,
        in_specs=placed,
        out_specs=P(AXES, None),
        check_vma=False,
    )
```

time: 68.3 us -> 56.1 us (0.82)
  the two profiles are of different devices: /device:TPU:25 before, /device:TPU:0 now
where the time goes in v1:
time: 56.1 us; the launch traced here: 55.6 us
  Pallas kernels  19.2 us (34%)
  waiting for transfers between devices  18 us (32%)
  starting transfers between devices  14.8 us (26%)
  local copies, waits for them, and re-layouts  3.41 us (6%)
    ppermute x15, waiting for transfers between devices, ahead(): lax.ppermute(array, axis, [((i + by) % length, i) for i in range(length)])  18 us
    ppermute x15, starting transfers between devices, ahead(): lax.ppermute(array, axis, [((i + by) % length, i) for i in range(length)])  14.8 us
    pallas_call x1, Pallas kernels, first_of(): pl.pallas_call(functools.partial(first_kernel, chips, depths), out_shape=...  5.29 us
    pallas_call x2, Pallas kernels, next_of(): pl.pallas_call(functools.partial(next_kernel, chips, depths, first, last)...  4.99 us
    pallas_call x3, Pallas kernels, message_of(): pl.pallas_call(message_kernel, out_shape=jax.ShapeDtypeStruct((rows + EXT...  4.05 us
    pallas_call x1, Pallas kernels, scores_of(): pl.pallas_call(score_kernel, out_shape=(jax.ShapeDtypeStruct((rows, heads...  3.49 us
    unnamed x13, local copies, waits for them, and re-layouts  3.41 us
    pallas_call x1, Pallas kernels, links_of(): pl.pallas_call(link_kernel, out_shape=jax.ShapeDtypeStruct((tile, tile),...  1.39 us
  transfers between devices with their start and end apart: 15, of which 4 were waited for; matrix products, arithmetic and copies ran while one was open for 2% of the time, Pallas kernels for 29%

profile of v1, /device:TPU:0, one launch (start us, length us, event | category | flops | bytes accessed | tf_op | source)
XLA Modules:
  0.0 55.6 jit_solution(16641120249275887854)
XLA Ops:
  0.0 7.0 %collective-permute-start.1 = (bf16[128,768]{1,0:T(8,128)(2,1)}, bf16[128,768]{1,0:T(8,128)(2,1)S(1)}, u32[]{:S(2)}, u32[]{:S(2)}) collective-permute-start(bf16[128,768]{1,0:T(8,128)(2,1)} %features_ref.1), channel_id=1, source_target_pairs={{2,0},{3,1},{4,2},{5,3},{6,4},{7,5},{8,6},{9,7},{10,8},{11,9},{12,... | collective-permute-start | bytes 589832 | tf_op jit(solution)/shard_map/ppermute | solution.py:28
  7.0 0.0 collective-permute-start.3
  7.0 3.5 %scores.1 = (f32[128,4]{1,0:T(8,128)S(1)}, bf16[136,768]{1,0:T(8,128)(2,1)S(1)}) custom-call(bf16[128,768]{1,0:T(8,128)(2,1)} %features_ref.1, bf16[768,3072]{1,0:T(8,128)(2,1)} %refs_3_.1, bf16[4,768]{1,0:T(4,128)(2,1)} %src_ref.1, bf16[4,768]{1,0:T(4,128)(2,1)} %dst_ref.7), custom_call_target="tpu_custom_call" | custom-call | flops 128 | bytes 128 | tf_op jit(solution)/shard_map/scores/pallas_call | solution.py:255
  10.5 0.6 %collective-permute-start.7 = (bf16[136,768]{1,0:T(8,128)(2,1)S(1)}, bf16[136,768]{1,0:T(8,128)(2,1)S(1)}, u32[]{:S(2)}, u32[]{:S(2)}) collective-permute-start(bf16[136,768]{1,0:T(8,128)(2,1)S(1)} %get-tuple-element.14.refs_0_), channel_id=1, source_target_pairs={{8,0},{16,8},{24,16},{0,24},{9,1},{17,9},{25,17},{1,25},{10,2},{18... | collective-permute-start | bytes 626696 | tf_op jit(solution)/shard_map/ppermute | solution.py:28
  11.1 1.9 %collective-permute-start.5 = (bf16[128,768]{1,0:T(8,128)(2,1)S(1)}, bf16[128,768]{1,0:T(8,128)(2,1)S(1)}, u32[]{:S(2)}, u32[]{:S(2)}) collective-permute-start(bf16[128,768]{1,0:T(8,128)(2,1)S(1)} %copy-done.5), channel_id=1, source_target_pairs={{6,0},{7,1},{8,2},{9,3},{10,4},{11,5},{12,6},{13,7},{14,8},{15,9},... | collective-permute-start | bytes 589832 | tf_op jit(solution)/shard_map/ppermute | solution.py:28
  13.0 0.0 collective-permute-start
  13.0 0.0 collective-permute-done.1.features_ref
  13.0 1.3 %message.3.refs_2_ = bf16[136,768]{1,0:T(8,128)(2,1)S(1)} custom-call(bf16[128,768]{1,0:T(8,128)(2,1)S(1)} %collective-permute-done.1.features_ref, bf16[768,3072]{1,0:T(8,128)(2,1)S(1)} %copy-done, bf16[4,768]{1,0:T(4,128)(2,1)S(1)} %copy-done.2), custom_call_target="tpu_custom_call" | custom-call | flops 603979776 | bytes 4718592 | tf_op jit(solution)/shard_map/message/pallas_call | solution.py:280
  14.4 0.5 collective-permute-start.2
  14.9 7.5 %collective-permute-done.3.features_ref = bf16[128,768]{1,0:T(8,128)(2,1)S(1)} collective-permute-done((bf16[128,768]{1,0:T(8,128)(2,1)}, bf16[128,768]{1,0:T(8,128)(2,1)S(1)}, u32[]{:S(2)}, u32[]{:S(2)}) %collective-permute-start.3) | collective-permute-done | bytes 196640 | tf_op jit(solution)/shard_map/ppermute | solution.py:28
  22.4 1.4 %message.4.refs_4_ = bf16[136,768]{1,0:T(8,128)(2,1)S(1)} custom-call(bf16[128,768]{1,0:T(8,128)(2,1)S(1)} %collective-permute-done.3.features_ref, bf16[768,3072]{1,0:T(8,128)(2,1)S(1)} %copy-done, bf16[4,768]{1,0:T(4,128)(2,1)S(1)} %copy-done.2), custom_call_target="tpu_custom_call" | custom-call | flops 603979776 | bytes 4718592 | tf_op jit(solution)/shard_map/message/pallas_call | solution.py:280
  23.8 0.0 copy-start.4
  23.8 0.1 collective-permute-start.4
  23.9 2.1 %collective-permute-start.9 = (bf16[136,768]{1,0:T(8,128)(2,1)S(1)}, bf16[136,768]{1,0:T(8,128)(2,1)S(1)}, u32[]{:S(2)}, u32[]{:S(2)}) collective-permute-start(bf16[136,768]{1,0:T(8,128)(2,1)S(1)} %message.3.refs_2_), channel_id=1, source_target_pairs={{8,0},{16,8},{24,16},{0,24},{9,1},{17,9},{25,17},{1,25},{10,2},{18... | collective-permute-start | bytes 626696 | tf_op jit(solution)/shard_map/ppermute | solution.py:28
  26.0 0.0 collective-permute-done.7.refs_8_
  26.0 0.5 collective-permute-start.11
  26.6 1.3 %message.5.refs_6_ = bf16[136,768]{1,0:T(8,128)(2,1)S(1)} custom-call(bf16[128,768]{1,0:T(8,128)(2,1)S(1)} %collective-permute-done.5.features_ref, bf16[768,3072]{1,0:T(8,128)(2,1)S(1)} %copy-done, bf16[4,768]{1,0:T(4,128)(2,1)S(1)} %copy-done.2), custom_call_target="tpu_custom_call" | custom-call | flops 603979776 | bytes 4718592 | tf_op jit(solution)/shard_map/message/pallas_call | solution.py:280
  27.9 0.0 collective-permute-done.refs_1_
  28.0 1.5 %collective-permute-start.13 = (bf16[136,768]{1,0:T(8,128)(2,1)S(1)}, bf16[136,768]{1,0:T(8,128)(2,1)S(1)}, u32[]{:S(2)}, u32[]{:S(2)}) collective-permute-start(bf16[136,768]{1,0:T(8,128)(2,1)S(1)} %message.5.refs_6_), channel_id=1, source_target_pairs={{8,0},{16,8},{24,16},{0,24},{9,1},{17,9},{25,17},{1,25},{10,2},{18... | collective-permute-start | bytes 626696 | tf_op jit(solution)/shard_map/ppermute | solution.py:28
  29.4 0.0 collective-permute-done.2.refs_3_
  29.4 0.0 collective-permute-start.6
  29.4 0.5 collective-permute-start.8
  30.0 2.0 %collective-permute-done.9.refs_3_ = bf16[136,768]{1,0:T(8,128)(2,1)S(1)} collective-permute-done((bf16[136,768]{1,0:T(8,128)(2,1)S(1)}, bf16[136,768]{1,0:T(8,128)(2,1)S(1)}, u32[]{:S(2)}, u32[]{:S(2)}) %collective-permute-start.9) | collective-permute-done | bytes 208928 | tf_op jit(solution)/shard_map/ppermute | solution.py:28
  32.0 4.5 %collective-permute-done.11.refs_5_ = bf16[136,768]{1,0:T(8,128)(2,1)S(1)} collective-permute-done((bf16[136,768]{1,0:T(8,128)(2,1)S(1)}, bf16[136,768]{1,0:T(8,128)(2,1)S(1)}, u32[]{:S(2)}, u32[]{:S(2)}) %collective-permute-start.11) | collective-permute-done | bytes 208928 | tf_op jit(solution)/shard_map/ppermute | solution.py:28
  36.5 3.9 %collective-permute-done.13.refs_4_ = bf16[136,768]{1,0:T(8,128)(2,1)S(1)} collective-permute-done((bf16[136,768]{1,0:T(8,128)(2,1)S(1)}, bf16[136,768]{1,0:T(8,128)(2,1)S(1)}, u32[]{:S(2)}, u32[]{:S(2)}) %collective-permute-start.13) | collective-permute-done | bytes 208928 | tf_op jit(solution)/shard_map/ppermute | solution.py:28
  40.4 1.0 %copy.8.near_ref = s32[1024,16]{1,0:T(8,128)S(1)} copy(s32[1024,16]{0,1:T(8,128)} %param.13) | data formatting | bytes 131072 | tf_op args[6]
  41.5 1.4 %links.1.link_ref = s32[128,128]{1,0:T(8,128)S(1)} custom-call(s32[8,8]{1,0:T(8,128)S(1)} %copy-done.3, s32[8]{0:T(128)S(1)} %copy-done.4, s32[1024,16]{1,0:T(8,128)S(1)} %copy.8.near_ref), custom_call_target="tpu_custom_call" | custom-call | flops 128 | bytes 128 | tf_op jit(solution)/shard_map/links/pallas_call | solution.py:294
  42.9 5.3 %first.1 = (f32[128,4]{1,0:T(8,128)S(1)}, f32[128,4]{1,0:T(8,128)S(1)}, f32[512,768]{1,0:T(8,128)S(1)}) custom-call(s32[8,8]{1,0:T(8,128)S(1)} %copy-done.3, s32[8]{0:T(128)S(1)} %copy-done.4, f32[128,4]{1,0:T(8,128)S(1)} %get-tuple-element.13.source_ref, s32[128,128]{1,0:T(8,128)S(1)} %links.1.link_ref, bf16[136,768]{1,0:T(8,128)(2,1)S(1)} %get-tuple-element.14.refs_0_, ...), custom_call_target="tpu_custom_call" | custom-call | flops 805306368 | bytes 3145728 | tf_op jit(solution)/shard_map/first/pallas_call | solution.py:323
  48.2 1.8 %middle.1 = (f32[128,4]{1,0:T(8,128)S(1)}, f32[128,4]{1,0:T(8,128)S(1)}, f32[512,768]{1,0:T(8,128)S(1)}) custom-call(s32[8,8]{1,0:T(8,128)S(1)} %copy-done.3, s32[8]{0:T(128)S(1)} %copy-done.4, f32[128,4]{1,0:T(8,128)S(1)} %get-tuple-element.13.source_ref, s32[128,128]{1,0:T(8,128)S(1)} %links.1.link_ref, f32[128,4]{1,0:T(8,128)S(1)} %get-tuple-element.15.refs_0_, ...), custom_call_target="tpu_custom_call" | custom-call | flops 402653184 | bytes 3145728 | tf_op jit(solution)/shard_map/middle/pallas_call | solution.py:349
  50.1 0.0 copy-start.1
  50.1 2.3 %copy-done.1 = bf16[768,3072]{1,0:T(8,128)(2,1)S(1)} copy-done((bf16[768,3072]{1,0:T(8,128)(2,1)S(1)}, bf16[768,3072]{1,0:T(8,128)(2,1)}, u32[]{:S(2)}) %copy-start.1) | copy-done | bytes 4718616
  52.4 3.2 %final.1 = bf16[128,768]{1,0:T(8,128)(2,1)} custom-call(s32[8,8]{1,0:T(8,128)S(1)} %copy-done.3, s32[8]{0:T(128)S(1)} %copy-done.4, f32[128,4]{1,0:T(8,128)S(1)} %get-tuple-element.13.source_ref, s32[128,128]{1,0:T(8,128)S(1)} %links.1.link_ref, f32[128,4]{1,0:T(8,128)S(1)} %get-tuple-element.18.refs_0_, f32[128,4]{1,0:T(8,128)S(1)} %get-tuple-element.19.refs_1_, ...), custom_call_target="tpu_custom_call" | custom-call | flops 805306368 | bytes 3145728 | tf_op jit(solution)/shard_map/final/pallas_call | solution.py:349
  (19 shorter events, 0.0 us)
Async XLA Ops:
  0.0 11.1 %copy-start.5 = (bf16[128,768]{1,0:T(8,128)(2,1)S(1)}, bf16[128,768]{1,0:T(8,128)(2,1)}, u32[]{:S(2)}) copy-start(bf16[128,768]{1,0:T(8,128)(2,1)} %features_ref.1) | copy-start | bytes 589828
  0.0 13.0 %copy-start.2 = (bf16[4,768]{1,0:T(4,128)(2,1)S(1)}, bf16[4,768]{1,0:T(4,128)(2,1)}, u32[]{:S(2)}) copy-start(bf16[4,768]{1,0:T(4,128)(2,1)} %dst_ref.7) | copy-start | bytes 18436
  0.0 13.0 %copy-start = (bf16[768,3072]{1,0:T(8,128)(2,1)S(1)}, bf16[768,3072]{1,0:T(8,128)(2,1)}, u32[]{:S(2)}) copy-start(bf16[768,3072]{1,0:T(8,128)(2,1)} %refs_3_.1) | copy-start | bytes 14155780
  0.0 13.0 %collective-permute-start.1 = (bf16[128,768]{1,0:T(8,128)(2,1)}, bf16[128,768]{1,0:T(8,128)(2,1)S(1)}, u32[]{:S(2)}, u32[]{:S(2)}) collective-permute-start(bf16[128,768]{1,0:T(8,128)(2,1)} %features_ref.1), channel_id=1, source_target_pairs={{2,0},{3,1},{4,2},{5,3},{6,4},{7,5},{8,6},{9,7},{10,8},{11,9},{12,... | collective-permute-start | bytes 589832 | tf_op jit(solution)/shard_map/ppermute | solution.py:28
  7.0 15.4 %collective-permute-start.3 = (bf16[128,768]{1,0:T(8,128)(2,1)}, bf16[128,768]{1,0:T(8,128)(2,1)S(1)}, u32[]{:S(2)}, u32[]{:S(2)}) collective-permute-start(bf16[128,768]{1,0:T(8,128)(2,1)} %features_ref.1), channel_id=1, source_target_pairs={{4,0},{5,1},{6,2},{7,3},{8,4},{9,5},{10,6},{11,7},{12,8},{13,9},{1... | collective-permute-start | bytes 589832 | tf_op jit(solution)/shard_map/ppermute | solution.py:28
  10.5 15.5 %collective-permute-start.7 = (bf16[136,768]{1,0:T(8,128)(2,1)S(1)}, bf16[136,768]{1,0:T(8,128)(2,1)S(1)}, u32[]{:S(2)}, u32[]{:S(2)}) collective-permute-start(bf16[136,768]{1,0:T(8,128)(2,1)S(1)} %get-tuple-element.14.refs_0_), channel_id=1, source_target_pairs={{8,0},{16,8},{24,16},{0,24},{9,1},{17,9},{25,17},{1,25},{10,2},{18... | collective-permute-start | bytes 626696 | tf_op jit(solution)/shard_map/ppermute | solution.py:28
  11.1 12.8 %collective-permute-start.5 = (bf16[128,768]{1,0:T(8,128)(2,1)S(1)}, bf16[128,768]{1,0:T(8,128)(2,1)S(1)}, u32[]{:S(2)}, u32[]{:S(2)}) collective-permute-start(bf16[128,768]{1,0:T(8,128)(2,1)S(1)} %copy-done.5), channel_id=1, source_target_pairs={{6,0},{7,1},{8,2},{9,3},{10,4},{11,5},{12,6},{13,7},{14,8},{15,9},... | collective-permute-start | bytes 589832 | tf_op jit(solution)/shard_map/ppermute | solution.py:28
  13.0 14.9 %collective-permute-start = (bf16[136,768]{1,0:T(8,128)(2,1)S(1)}, bf16[136,768]{1,0:T(8,128)(2,1)S(1)}, u32[]{:S(2)}, u32[]{:S(2)}) collective-permute-start(bf16[136,768]{1,0:T(8,128)(2,1)S(1)} %get-tuple-element.14.refs_0_), channel_id=1, source_target_pairs={{1,0},{0,1},{3,2},{2,3},{5,4},{4,5},{7,6},{6,7},{9,8},{8,9},{11,10... | collective-permute-start | bytes 626696 | tf_op jit(solution)/shard_map/ppermute | solution.py:28
  14.4 15.1 %collective-permute-start.2 = (bf16[136,768]{1,0:T(8,128)(2,1)S(1)}, bf16[136,768]{1,0:T(8,128)(2,1)S(1)}, u32[]{:S(2)}, u32[]{:S(2)}) collective-permute-start(bf16[136,768]{1,0:T(8,128)(2,1)S(1)} %message.3.refs_2_), channel_id=1, source_target_pairs={{1,0},{0,1},{3,2},{2,3},{5,4},{4,5},{7,6},{6,7},{9,8},{8,9},{11,10... | collective-permute-start | bytes 626696 | tf_op jit(solution)/shard_map/ppermute | solution.py:28
  23.8 17.7 %copy-start.3 = (s32[8,8]{1,0:T(8,128)S(1)}, s32[8,8]{1,0:T(8,128)}, u32[]{:S(2)}) copy-start(s32[8,8]{1,0:T(8,128)} %cols_ref.7) | copy-start | bytes 772
  23.8 17.7 %copy-start.4 = (s32[8]{0:T(128)S(1)}, s32[8]{0:T(128)}, u32[]{:S(2)}) copy-start(s32[8]{0:T(128)} %count_ref.7) | copy-start | bytes 100
  23.8 5.6 %collective-permute-start.4 = (bf16[136,768]{1,0:T(8,128)(2,1)S(1)}, bf16[136,768]{1,0:T(8,128)(2,1)S(1)}, u32[]{:S(2)}, u32[]{:S(2)}) collective-permute-start(bf16[136,768]{1,0:T(8,128)(2,1)S(1)} %message.4.refs_4_), channel_id=1, source_target_pairs={{1,0},{0,1},{3,2},{2,3},{5,4},{4,5},{7,6},{6,7},{9,8},{8,9},{11,10... | collective-permute-start | bytes 626696 | tf_op jit(solution)/shard_map/ppermute | solution.py:28
  23.9 8.1 %collective-permute-start.9 = (bf16[136,768]{1,0:T(8,128)(2,1)S(1)}, bf16[136,768]{1,0:T(8,128)(2,1)S(1)}, u32[]{:S(2)}, u32[]{:S(2)}) collective-permute-start(bf16[136,768]{1,0:T(8,128)(2,1)S(1)} %message.3.refs_2_), channel_id=1, source_target_pairs={{8,0},{16,8},{24,16},{0,24},{9,1},{17,9},{25,17},{1,25},{10,2},{18... | collective-permute-start | bytes 626696 | tf_op jit(solution)/shard_map/ppermute | solution.py:28
  26.0 10.4 %collective-permute-start.11 = (bf16[136,768]{1,0:T(8,128)(2,1)S(1)}, bf16[136,768]{1,0:T(8,128)(2,1)S(1)}, u32[]{:S(2)}, u32[]{:S(2)}) collective-permute-start(bf16[136,768]{1,0:T(8,128)(2,1)S(1)} %message.4.refs_4_), channel_id=1, source_target_pairs={{8,0},{16,8},{24,16},{0,24},{9,1},{17,9},{25,17},{1,25},{10,2},{18... | collective-permute-start | bytes 626696 | tf_op jit(solution)/shard_map/ppermute | solution.py:28
  28.0 12.5 %collective-permute-start.13 = (bf16[136,768]{1,0:T(8,128)(2,1)S(1)}, bf16[136,768]{1,0:T(8,128)(2,1)S(1)}, u32[]{:S(2)}, u32[]{:S(2)}) collective-permute-start(bf16[136,768]{1,0:T(8,128)(2,1)S(1)} %message.5.refs_6_), channel_id=1, source_target_pairs={{8,0},{16,8},{24,16},{0,24},{9,1},{17,9},{25,17},{1,25},{10,2},{18... | collective-permute-start | bytes 626696 | tf_op jit(solution)/shard_map/ppermute | solution.py:28
  29.4 13.5 %collective-permute-start.6 = (bf16[136,768]{1,0:T(8,128)(2,1)S(1)}, bf16[136,768]{1,0:T(8,128)(2,1)}, u32[]{:S(2)}, u32[]{:S(2)}) collective-permute-start(bf16[136,768]{1,0:T(8,128)(2,1)S(1)} %message.5.refs_6_), channel_id=1, source_target_pairs={{1,0},{0,1},{3,2},{2,3},{5,4},{4,5},{7,6},{6,7},{9,8},{8,9},{11,10... | collective-permute-start | bytes 626696 | tf_op jit(solution)/shard_map/ppermute | solution.py:28
  29.4 13.5 %collective-permute-start.8 = (bf16[136,768]{1,0:T(8,128)(2,1)S(1)}, bf16[136,768]{1,0:T(8,128)(2,1)}, u32[]{:S(2)}, u32[]{:S(2)}) collective-permute-start(bf16[136,768]{1,0:T(8,128)(2,1)S(1)} %collective-permute-done.7.refs_8_), channel_id=1, source_target_pairs={{1,0},{0,1},{3,2},{2,3},{5,4},{4,5},{7,6},{6,7},{9,8},{8,9},{11,10... | collective-permute-start | bytes 626696 | tf_op jit(solution)/shard_map/ppermute | solution.py:28
  32.0 16.2 %collective-permute-start.10 = (bf16[136,768]{1,0:T(8,128)(2,1)S(1)}, bf16[136,768]{1,0:T(8,128)(2,1)S(1)}, u32[]{:S(2)}, u32[]{:S(2)}) collective-permute-start(bf16[136,768]{1,0:T(8,128)(2,1)S(1)} %collective-permute-done.9.refs_3_), channel_id=1, source_target_pairs={{1,0},{0,1},{3,2},{2,3},{5,4},{4,5},{7,6},{6,7},{9,8},{8,9},{11,10... | collective-permute-start | bytes 626696 | tf_op jit(solution)/shard_map/ppermute | solution.py:28
  36.5 11.7 %collective-permute-start.12 = (bf16[136,768]{1,0:T(8,128)(2,1)S(1)}, bf16[136,768]{1,0:T(8,128)(2,1)S(1)}, u32[]{:S(2)}, u32[]{:S(2)}) collective-permute-start(bf16[136,768]{1,0:T(8,128)(2,1)S(1)} %collective-permute-done.11.refs_5_), channel_id=1, source_target_pairs={{1,0},{0,1},{3,2},{2,3},{5,4},{4,5},{7,6},{6,7},{9,8},{8,9},{11,10... | collective-permute-start | bytes 626696 | tf_op jit(solution)/shard_map/ppermute | solution.py:28
  40.4 9.6 %collective-permute-start.14 = (bf16[136,768]{1,0:T(8,128)(2,1)S(1)}, bf16[136,768]{1,0:T(8,128)(2,1)S(1)}, u32[]{:S(2)}, u32[]{:S(2)}) collective-permute-start(bf16[136,768]{1,0:T(8,128)(2,1)S(1)} %collective-permute-done.13.refs_4_), channel_id=1, source_target_pairs={{1,0},{0,1},{3,2},{2,3},{5,4},{4,5},{7,6},{6,7},{9,8},{8,9},{11,10... | collective-permute-start | bytes 626696 | tf_op jit(solution)/shard_map/ppermute | solution.py:28
  50.1 2.3 %copy-start.1 = (bf16[768,3072]{1,0:T(8,128)(2,1)S(1)}, bf16[768,3072]{1,0:T(8,128)(2,1)}, u32[]{:S(2)}) copy-start(bf16[768,3072]{1,0:T(8,128)(2,1)} %refs_3_.1) | copy-start | bytes 14155780
